TPU v7x, 512 devices: a whole 4x8x8 slice. The times are simulated.
512 devices in a mesh: req: 64 (over x, z, core), tp: 8 (over y).
Axes of the slice: x: 4, y: 8, z: 8, core: 2. Of those that a mesh axis runs over, the one named last changes fastest.
Arguments:
- queries: bfloat16 [4, 512, 1024], P(None, 'req', 'tp'), may hold values from -6 to 6
- new_kv: bfloat16 [4, 512, 2, 1024], P(None, 'req', None, 'tp'), may hold values from -4 to 4
- residual: bfloat16 [4, 512, 2048], P(None, 'req'), may hold values from -1.1953125 to 1.1953125
- home_cache: bfloat16 [256, 128, 2, 1024], P('req', None, None, 'tp'), may hold values from -6 to 6
- prompt_cache: bfloat16 [256, 128, 2, 1024], P('req', None, None, 'tp'), may hold values from -6 to 6
- home_table: int32 [512, 4], P('req'), may hold values from 0 to 3
- home_len: int32 [512], P('req'), may hold values from 1 to 512, as said below
- parents: int32 [4, 512], P(None, 'req'), may hold values from 0 to 7
- prompt_place: int32 [64], P('req'), may hold values from 0 to 63, as said below
- owned_request: int32 [64], P('req'), may hold values from 0 to 63, as said below
- prompt_len: int32 [64], P('req'), may hold values from 1 to 512, as said below
- out_weight: bfloat16 [1024, 2048], P('tp'), may hold values from -0.1875 to 0.1875
- norm_gain: bfloat16 [2048], replicated, may hold values from 0.099609375 to 1.8984375
- qkv_weight: bfloat16 [2048, 3, 1024], P(None, None, 'tp'), may hold values from -0.03125 to 0.03125
Outputs:
- next_qkv: bfloat16 [4, 512, 3, 1024], P(None, 'req', None, 'tp')
- new_residual: bfloat16 [4, 512, 2048], P(None, 'req')
Inputs may be any that keep to these rules, and one draw needn't show every extreme that they name: `home_len`: some beam has all 512 tokens. `prompt_len`: some prompt has all 512 tokens. `prompt_place`: A permutation. Slot j lies on device j. The 1 request of one device have their prompts on 1 different devices, each device holds prompts of 1 request of different devices, and a request's position among its device's requests equals its slot's position j % 1. `owned_request`: the inverse permutation of prompt_place.
All inputs are finite; a program needn't handle non-finite values.
Results may differ from a plain program's by a relative error of at most 0.013.
Values may be sent and summed in bfloat16 or wider, within the bound.
No kernel may reach another device: no remote copies, remote signals or barrier semaphores. Data moves between devices by JAX's collectives and lax.ppermute only.
A program may use at most 64 MiB of HBM per device.

v0:
```python
import math
import jax
import jax.numpy as jnp
from jax import lax
from jax.sharding import PartitionSpec as P

HEAD_DIM = 64
BEAMS = 8
NEG_FILL = -1e30
NORM_EPS = 1e-05


def shards(
    queries,
    new_kv,
    residual,
    home_cache,
    prompt_cache,
    home_table,
    home_len,
    parents,
    prompt_place,
    owned_request,
    prompt_len,
    out_weight,
    norm_gain,
    qkv_weight,
):
    step_count, row_count, lane_count = queries.shape
    head_count = lane_count // HEAD_DIM
    request_count = row_count // BEAMS
    block_count = home_table.shape[1]
    block_size = home_cache.shape[1]
    prompt_tokens = prompt_cache.shape[0] * block_size // request_count
    home_tokens = block_count * block_size
    req_size = lax.axis_size("req")
    score_scale = 1.0 / math.sqrt(HEAD_DIM)
    request_base = jnp.arange(row_count, dtype=jnp.int32) // BEAMS * BEAMS
    first_parent = request_base + parents[0]
    tables = home_table[first_parent]
    lengths = home_len[first_parent]
    window = jnp.zeros((row_count, step_count, 2, lane_count), jnp.bfloat16)
    prompt_heads = prompt_cache.reshape(request_count, prompt_tokens, 2, head_count, HEAD_DIM)
    prompt_pos = jnp.arange(prompt_tokens, dtype=jnp.int32)
    home_pos = jnp.arange(home_tokens, dtype=jnp.int32)
    window_pos = jnp.arange(step_count, dtype=jnp.int32)
    gain_row = norm_gain.astype(jnp.float32)
    weight_flat = qkv_weight.reshape(qkv_weight.shape[0], 3 * lane_count)
    qkv_list = []
    residual_list = []
    for step_index in range(step_count):
        if step_index > 0:
            window = window.at[:, step_index - 1].set(new_kv[step_index - 1])
            chosen = request_base + parents[step_index]
            window = window[chosen]
            tables = tables[chosen]
            lengths = lengths[chosen]
        query_block = queries[step_index : step_index + 1]
        route_block_steps = query_block.shape[0]
        all_queries = lax.all_gather(query_block, "req", axis=1, tiled=True)
        route_query_held = all_queries.reshape(
            route_block_steps, req_size * request_count, BEAMS, head_count, HEAD_DIM
        )[:, owned_request]
        prompt_block_steps = route_query_held.shape[0]
        scores = (
            jnp.einsum(
                "krbhd,rthd->krbht",
                route_query_held,
                prompt_heads[:, :, 0],
                preferred_element_type=jnp.float32,
            )
            * score_scale
        )
        scores = jnp.where(
            prompt_pos[None, None, None, None, :] < prompt_len[None, :, None, None, None],
            scores,
            NEG_FILL,
        )
        row_top = jnp.max(scores, axis=-1)
        weights = jnp.exp(scores - row_top[..., None]).astype(jnp.bfloat16)
        weight_sum = jnp.sum(weights.astype(jnp.float32), axis=-1)
        numerator = jnp.einsum(
            "krbht,rthd->krbhd", weights, prompt_heads[:, :, 1], preferred_element_type=jnp.float32
        )
        held_numer = numerator.reshape(prompt_block_steps, row_count, lane_count)
        held_top = row_top.reshape(prompt_block_steps, row_count, head_count)
        held_sum = weight_sum.reshape(prompt_block_steps, row_count, head_count)
        all_numer = lax.all_gather(held_numer, "req", axis=1, tiled=True)
        all_top = lax.all_gather(held_top, "req", axis=1, tiled=True)
        all_sum_rows = lax.all_gather(held_sum, "req", axis=1, tiled=True)
        route_prompt_numer = all_numer.reshape(
            route_block_steps, req_size * request_count, BEAMS, lane_count
        )[:, prompt_place].reshape(route_block_steps, row_count, lane_count)
        route_prompt_top = all_top.reshape(
            route_block_steps, req_size * request_count, BEAMS, head_count
        )[:, prompt_place].reshape(route_block_steps, row_count, head_count)
        route_prompt_sum = all_sum_rows.reshape(
            route_block_steps, req_size * request_count, BEAMS, head_count
        )[:, prompt_place].reshape(route_block_steps, row_count, head_count)
        attend_prompt_numer = route_prompt_numer[0]
        attend_prompt_top = route_prompt_top[0]
        attend_prompt_sum = route_prompt_sum[0]
        query_heads = queries[step_index].reshape(row_count, head_count, HEAD_DIM)
        gathered = home_cache[tables].reshape(row_count, home_tokens, 2, head_count, HEAD_DIM)
        window_heads = window.reshape(row_count, step_count, 2, head_count, HEAD_DIM)
        own_heads = new_kv[step_index].reshape(row_count, 2, head_count, HEAD_DIM)
        home_scores = (
            jnp.einsum(
                "bhd,bthd->bht", query_heads, gathered[:, :, 0], preferred_element_type=jnp.float32
            )
            * score_scale
        )
        home_scores = jnp.where(
            home_pos[None, None, :] < lengths[:, None, None], home_scores, NEG_FILL
        )
        window_scores = (
            jnp.einsum(
                "bhd,bthd->bht",
                query_heads,
                window_heads[:, :, 0],
                preferred_element_type=jnp.float32,
            )
            * score_scale
        )
        window_scores = jnp.where(window_pos < step_index, window_scores, NEG_FILL)
        own_scores = (
            jnp.einsum(
                "bhd,bhd->bh", query_heads, own_heads[:, 0], preferred_element_type=jnp.float32
            )
            * score_scale
        )
        home_top = jnp.maximum(
            jnp.maximum(jnp.max(home_scores, axis=-1), jnp.max(window_scores, axis=-1)), own_scores
        )
        home_weights = jnp.exp(home_scores - home_top[..., None]).astype(jnp.bfloat16)
        window_weights = jnp.exp(window_scores - home_top[..., None]).astype(jnp.bfloat16)
        own_weights = jnp.exp(own_scores - home_top).astype(jnp.bfloat16)
        home_sum = (
            jnp.sum(home_weights.astype(jnp.float32), axis=-1)
            + jnp.sum(window_weights.astype(jnp.float32), axis=-1)
            + own_weights.astype(jnp.float32)
        )
        home_numer = jnp.einsum(
            "bht,bthd->bhd", home_weights, gathered[:, :, 1], preferred_element_type=jnp.float32
        )
        home_numer = home_numer + jnp.einsum(
            "bht,bthd->bhd",
            window_weights,
            window_heads[:, :, 1],
            preferred_element_type=jnp.float32,
        )
        home_numer = home_numer + own_weights.astype(jnp.float32)[..., None] * own_heads[
            :, 1
        ].astype(jnp.float32)
        attend_prompt_numer = attend_prompt_numer.reshape(row_count, head_count, HEAD_DIM)
        joint_top = jnp.maximum(home_top, attend_prompt_top)
        home_factor = jnp.exp(home_top - joint_top)
        prompt_factor = jnp.exp(attend_prompt_top - joint_top)
        joint_sum = home_sum * home_factor + attend_prompt_sum * prompt_factor
        joint_numer = (
            home_numer * home_factor[..., None] + attend_prompt_numer * prompt_factor[..., None]
        )
        attended = (
            (joint_numer / joint_sum[..., None]).astype(jnp.bfloat16).reshape(row_count, lane_count)
        )
        attended_block = attended[None]
        residual_block = residual[step_index : step_index + 1]
        block_steps = attended_block.shape[0]
        flat_rows = block_steps * row_count
        attended_flat = attended_block.reshape(flat_rows, lane_count)
        residual_flat = residual_block.reshape(flat_rows, residual_block.shape[-1])
        projected = jnp.dot(attended_flat, out_weight, preferred_element_type=jnp.float32)
        head_total = lax.psum(projected, "tp")
        mixed_rows = residual_flat.astype(jnp.float32) + head_total
        mean_square = jnp.mean(mixed_rows * mixed_rows, axis=-1, keepdims=True)
        normed = (mixed_rows * lax.rsqrt(mean_square + NORM_EPS) * gain_row).astype(jnp.bfloat16)
        residual_out = mixed_rows.astype(jnp.bfloat16)
        next_rows = jnp.dot(normed, weight_flat, preferred_element_type=jnp.float32).astype(
            jnp.bfloat16
        )
        qkv_step = next_rows.reshape(block_steps, row_count, 3, lane_count)
        residual_step = residual_out.reshape(block_steps, row_count, residual_out.shape[-1])
        qkv_list.append(qkv_step[0])
        residual_list.append(residual_step[0])
    return (jnp.stack(qkv_list), jnp.stack(residual_list))


def solution(mesh):
    placed = (
        P(None, "req", "tp"),
        P(None, "req", None, "tp"),
        P(None, "req", None),
        P("req", None, None, "tp"),
        P("req", None, None, "tp"),
        P("req", None),
        P("req"),
        P(None, "req"),
        P("req"),
        P("req"),
        P("req"),
        P("tp", None),
        P(),
        P(None, None, "tp"),
    )
    return jax.shard_map(
        shards,
        mesh=mesh,
        in_specs=placed,
        out_specs=(P(None, "req", None, "tp"), P(None, "req", None)),
        check_vma=False,
    )
```

profile of v0, /device:TPU:2, one launch (start us, length us, event | category | flops | bytes accessed | tf_op | source)
XLA Modules:
  0.0 910.0 jit_solution(6705653716037907314)
XLA Ops:
  12.4 6.4 gather_fusion.9
  18.8 2.8 copy.172
  21.6 3.1 reshape.675
  24.7 1.4 slice_bitcast_fusion.3
  30.8 1.9 fusion.22
  33.4 1.3 convert_reduce_fusion.3
  34.7 1.2 convert_reduce_fusion.9
  35.9 55.4 %all_gather.56 = bf16[1,512,128]{2,1,0:T(8,128)(2,1)S(1)} all-gather(bf16[1,8,128]{2,1,0:T(8,128)(2,1)S(1)} %get-tuple-element.276), channel_id=1, replica_groups=mesh['req'=64,'tp'=8] {'req'}, dimensions={1}, use_global_device_ids=true | all-gather | bytes 133120 | tf_op jit(solution)/shard_map/all_gather | solution.py:60
  92.8 48.2 %all_gather.60 = bf16[1,512,128]{2,1,0:T(8,128)(2,1)S(1)} all-gather(bf16[1,8,128]{2,1,0:T(8,128)(2,1)S(1)} %get-tuple-element.279), channel_id=1, replica_groups=mesh['req'=64,'tp'=8] {'req'}, dimensions={1}, use_global_device_ids=true | all-gather | bytes 133120 | tf_op jit(solution)/shard_map/all_gather | solution.py:60
  145.0 5.4 gather_fusion.13
  150.4 2.8 copy.181
  153.2 3.1 reshape.687
  156.3 1.4 slice_bitcast_fusion.1
  159.1 1.9 fusion.18
  161.7 1.3 convert_reduce_fusion.1
  162.9 1.2 convert_reduce_fusion.8
  167.7 5.4 gather_fusion.5
  173.1 2.8 copy.163
  175.9 3.1 reshape.663
  179.0 1.2 slice_bitcast_fusion.5
  181.6 1.3 convert_reduce_fusion.5
  182.8 1.2 convert_reduce_fusion.10
  184.1 48.3 %all_gather.52 = bf16[1,512,128]{2,1,0:T(8,128)(2,1)S(1)} all-gather(bf16[1,8,128]{2,1,0:T(8,128)(2,1)S(1)} %get-tuple-element.277), channel_id=1, replica_groups=mesh['req'=64,'tp'=8] {'req'}, dimensions={1}, use_global_device_ids=true | all-gather | bytes 133120 | tf_op jit(solution)/shard_map/all_gather | solution.py:60
  232.3 47.7 %all_gather.48 = bf16[1,512,128]{2,1,0:T(8,128)(2,1)S(1)} all-gather(bf16[1,8,128]{2,1,0:T(8,128)(2,1)S(1)} %get-tuple-element.278), channel_id=1, replica_groups=mesh['req'=64,'tp'=8] {'req'}, dimensions={1}, use_global_device_ids=true | all-gather | bytes 133120 | tf_op jit(solution)/shard_map/all_gather | solution.py:60
  281.8 0.9 fusion.154
  283.3 0.9 fusion.153
  284.6 42.4 %all-gather.13 = f32[64,8,2]{1,2,0:T(2,128)S(1)} all-gather(f32[1,8,2]{1,2,0:T(2,128)} %bitcast.533), channel_id=7, replica_groups=mesh['req'=64,'tp'=8] {'req'}, dimensions={0}, use_global_device_ids=true | all-gather | bytes 4160 | tf_op jit(solution)/shard_map/all_gather | solution.py:90
  327.0 41.3 %all-gather.12 = f32[64,8,2]{1,2,0:T(2,128)S(1)} all-gather(f32[1,8,2]{1,2,0:T(2,128)S(1)} %bitcast.517), channel_id=6, replica_groups=mesh['req'=64,'tp'=8] {'req'}, dimensions={0}, use_global_device_ids=true | all-gather | bytes 4160 | tf_op jit(solution)/shard_map/all_gather | solution.py:89
  370.9 43.2 %all_gather.58 = f32[1,512,128]{2,1,0:T(8,128)S(1)} all-gather(f32[1,8,128]{2,1,0:T(8,128)S(1)} %reshape.683), channel_id=1, replica_groups=mesh['req'=64,'tp'=8] {'req'}, dimensions={1}, use_global_device_ids=true | all-gather | bytes 266240 | tf_op jit(solution)/shard_map/all_gather | solution.py:88
  414.2 1.4 fusion.20
  416.7 41.3 %all-gather.15 = f32[64,8,2]{1,2,0:T(2,128)S(1)} all-gather(f32[1,8,2]{1,2,0:T(2,128)} %bitcast.534), channel_id=9, replica_groups=mesh['req'=64,'tp'=8] {'req'}, dimensions={0}, use_global_device_ids=true | all-gather | bytes 4160 | tf_op jit(solution)/shard_map/all_gather | solution.py:90
  458.0 42.8 %all-gather.14 = f32[64,8,2]{1,2,0:T(2,128)S(1)} all-gather(f32[1,8,2]{1,2,0:T(2,128)} %bitcast.518), channel_id=8, replica_groups=mesh['req'=64,'tp'=8] {'req'}, dimensions={0}, use_global_device_ids=true | all-gather | bytes 4160 | tf_op jit(solution)/shard_map/all_gather | solution.py:89
  503.4 41.7 %all_gather.62 = f32[1,512,128]{2,1,0:T(8,128)S(1)} all-gather(f32[1,8,128]{2,1,0:T(8,128)S(1)} %reshape.695), channel_id=1, replica_groups=mesh['req'=64,'tp'=8] {'req'}, dimensions={1}, use_global_device_ids=true | all-gather | bytes 266240 | tf_op jit(solution)/shard_map/all_gather | solution.py:88
  547.9 42.8 %all-gather.11 = f32[64,8,2]{1,2,0:T(2,128)S(1)} all-gather(f32[1,8,2]{1,2,0:T(2,128)S(1)} %bitcast.535), channel_id=5, replica_groups=mesh['req'=64,'tp'=8] {'req'}, dimensions={0}, use_global_device_ids=true | all-gather | bytes 4160 | tf_op jit(solution)/shard_map/all_gather | solution.py:90
  590.7 41.3 %all-gather.10 = f32[64,8,2]{1,2,0:T(2,128)S(1)} all-gather(f32[1,8,2]{1,2,0:T(2,128)S(1)} %bitcast.519), channel_id=4, replica_groups=mesh['req'=64,'tp'=8] {'req'}, dimensions={0}, use_global_device_ids=true | all-gather | bytes 4160 | tf_op jit(solution)/shard_map/all_gather | solution.py:89
  632.6 43.4 %all_gather.54 = f32[1,512,128]{2,1,0:T(8,128)S(1)} all-gather(f32[1,8,128]{2,1,0:T(8,128)S(1)} %reshape.671), channel_id=1, replica_groups=mesh['req'=64,'tp'=8] {'req'}, dimensions={1}, use_global_device_ids=true | all-gather | bytes 266240 | tf_op jit(solution)/shard_map/all_gather | solution.py:88
  678.1 5.4 gather_fusion.2
  683.5 2.8 copy.151
  686.3 3.1 reshape.649
  689.4 1.5 slice_bitcast_fusion.7
  691.2 1.9 fusion.30
  693.4 41.3 %all-gather.9 = f32[64,8,2]{1,2,0:T(2,128)S(1)} all-gather(f32[1,8,2]{1,2,0:T(2,128)S(1)} %bitcast.532), channel_id=3, replica_groups=mesh['req'=64,'tp'=8] {'req'}, dimensions={0}, use_global_device_ids=true | all-gather | bytes 4160 | tf_op jit(solution)/shard_map/all_gather | solution.py:90
  734.7 42.8 %all-gather.8 = f32[64,8,2]{1,2,0:T(2,128)S(1)} all-gather(f32[1,8,2]{1,2,0:T(2,128)S(1)} %bitcast.516), channel_id=2, replica_groups=mesh['req'=64,'tp'=8] {'req'}, dimensions={0}, use_global_device_ids=true | all-gather | bytes 4160 | tf_op jit(solution)/shard_map/all_gather | solution.py:89
  778.3 41.7 %all_gather.50 = f32[1,512,128]{2,1,0:T(8,128)S(1)} all-gather(f32[1,8,128]{2,1,0:T(8,128)S(1)} %reshape.658), channel_id=1, replica_groups=mesh['req'=64,'tp'=8] {'req'}, dimensions={1}, use_global_device_ids=true | all-gather | bytes 266240 | tf_op jit(solution)/shard_map/all_gather | solution.py:88
  821.8 1.7 copy.160
  823.5 73.9 %all-reduce.4.cloned.1.call-done = (f32[8,2048]{1,0:T(8,128)}, f32[8,2048]{1,0:T(8,128)}, f32[8,2048]{1,0:T(8,128)}, f32[8,2048]{1,0:T(8,128)}) async-done(((f32[8,2048]{1,0:T(8,128)}, f32[8,2048]{1,0:T(8,128)}, f32[8,2048]{1,0:T(8,128)}, f32[8,2048]{1,0:T(8,128)}), (f32[8,2048]{1,0:T(8,128)}, f32[8,2048]{1,0:T(8,128)}, f32[8,2048]{1,0:T(8,128)}, f32[8,2048]{1,0:T(8,128)})) %all-reduce.4.cloned.1.call-update) | async-done | bytes 262160 | tf_op jit(solution)/shard_map/psum | solution.py:173
  897.5 1.1 multiply_reduce_fusion.3
  898.6 1.3 fusion.12
  (260 shorter events, 41.1 us)
Async XLA Ops:
  7.2 539.1 %copy-start = (bf16[128,2048]{1,0:T(8,128)(2,1)S(1)}, bf16[128,2048]{1,0:T(8,128)(2,1)}, u32[]{:S(2)}) copy-start(bf16[128,2048]{1,0:T(8,128)(2,1)} %param.31) | copy-start | bytes 1572868
  7.2 890.3 %all-reduce.4.cloned.1.call-start = ((), (), s32[]{:S(2)}) async-start(), calls=%async_computation | async-start | bytes 524288 | tf_op jit(solution)/shard_map/psum | solution.py:173
  24.7 1.5 copy-start.1
  24.7 3.5 copy-start.12
  26.8 114.4 %copy-start.8 = (bf16[4,128,2,128]{3,2,1,0:T(2,128)(2,1)S(1)}, bf16[4,128,2,128]{3,2,1,0:T(2,128)(2,1)}, u32[]{:S(2)}) copy-start(bf16[4,128,2,128]{3,2,1,0:T(2,128)(2,1)} %param.24) | copy-start | bytes 786436
  30.8 114.2 %copy-start.2 = (bf16[4,128,2,128]{3,2,1,0:T(2,128)(2,1)S(1)}, bf16[4,128,2,128]{3,2,1,0:T(2,128)(2,1)}, u32[]{:S(2)}) copy-start(bf16[4,128,2,128]{3,2,1,0:T(2,128)(2,1)} %param.23) | copy-start | bytes 786436
  33.0 117.4 %copy-start.13 = (bf16[8,2,2,64]{3,2,1,0:T(2,128)(2,1)}, bf16[8,2,2,64]{3,2,1,0:T(2,128)(2,1)S(1)}, u32[]{:S(2)}) copy-start(bf16[8,2,2,64]{3,2,1,0:T(2,128)(2,1)S(1)} %reshape_squeeze.29) | copy-start | bytes 12292
  33.2 109.0 %copy-start.29 = (f32[8,2]{0,1:T(2,128)}, f32[8,2]{0,1:T(2,128)S(1)}, u32[]{:S(2)}) copy-start(f32[8,2]{0,1:T(2,128)S(1)} %copy.224) | copy-start | bytes 196
  33.4 117.0 %copy-start.19 = (f32[8,2]{0,1:T(2,128)}, f32[8,2]{0,1:T(2,128)S(1)}, u32[]{:S(2)}) copy-start(f32[8,2]{0,1:T(2,128)S(1)} %maximum_maximum_fusion.1) | copy-start | bytes 196
  142.1 22.0 %copy-start.33 = (pred[512]{0:T(512)(128)(4,1)}, pred[512]{0:T(512)(128)(4,1)S(1)}, u32[]{:S(2)}) copy-start(pred[512]{0:T(512)(128)(4,1)S(1)} %iota_compare_fusion.4) | copy-start | bytes 1540
  161.3 6.4 copy-start.14
  161.5 11.7 %copy-start.30 = (f32[8,2]{0,1:T(2,128)}, f32[8,2]{0,1:T(2,128)S(1)}, u32[]{:S(2)}) copy-start(f32[8,2]{0,1:T(2,128)S(1)} %copy.239) | copy-start | bytes 196
  161.7 6.0 copy-start.20
  164.4 3.3 copy-start.18
  180.2 234.0 %copy-start.3 = (bf16[8,512,2,64]{1,0,3,2:T(8,128)(2,1)S(1)}, bf16[8,512,2,64]{1,0,3,2:T(8,128)(2,1)}, u32[]{:S(2)}) copy-start(bf16[8,512,2,64]{1,0,3,2:T(8,128)(2,1)} %get-tuple-element.246) | copy-start | bytes 3145732
  181.2 1.7 copy-start.16
  181.4 1.5 copy-start.31
  181.6 1.3 copy-start.21
  184.1 361.2 %copy-start.4 = (bf16[8,512,2,64]{1,0,3,2:T(8,128)(2,1)S(1)}, bf16[8,512,2,64]{1,0,3,2:T(8,128)(2,1)}, u32[]{:S(2)}) copy-start(bf16[8,512,2,64]{1,0,3,2:T(8,128)(2,1)} %get-tuple-element.248) | copy-start | bytes 3145732
  281.1 134.6 %copy-start.26 = (bf16[8,4,2,64]{3,2,1,0:T(2,128)(2,1)S(1)}, bf16[8,4,2,64]{3,2,1,0:T(2,128)(2,1)}, u32[]{:S(2)}) copy-start(bf16[8,4,2,64]{3,2,1,0:T(2,128)(2,1)} %get-tuple-element.265) | copy-start | bytes 24580
  281.1 264.1 %copy-start.23 = (bf16[8,2,512,1]{2,0,1,3:T(8,128)(2,1)S(1)}, bf16[8,2,512,1]{2,0,1,3:T(8,128)(2,1)}, u32[]{:S(2)}) copy-start(bf16[8,2,512,1]{2,0,1,3:T(8,128)(2,1)} %get-tuple-element.260) | copy-start | bytes 49156
  282.9 263.1 %copy-start.28 = (bf16[8,4,2,64]{3,2,1,0:T(2,128)(2,1)S(1)}, bf16[8,4,2,64]{3,2,1,0:T(2,128)(2,1)}, u32[]{:S(2)}) copy-start(bf16[8,4,2,64]{3,2,1,0:T(2,128)(2,1)} %get-tuple-element.267) | copy-start | bytes 24580
  282.9 263.2 %copy-start.15 = (bf16[8,2,2,64]{3,2,1,0:T(2,128)(2,1)S(1)}, bf16[8,2,2,64]{3,2,1,0:T(2,128)(2,1)}, u32[]{:S(2)}) copy-start(bf16[8,2,2,64]{3,2,1,0:T(2,128)(2,1)} %copy-done.14) | copy-start | bytes 12292
  414.2 217.8 %copy-start.22 = (f32[8,2]{0,1:T(2,128)S(1)}, f32[8,2]{0,1:T(2,128)}, u32[]{:S(2)}) copy-start(f32[8,2]{0,1:T(2,128)} %copy-done.21) | copy-start | bytes 196
  414.2 217.8 %copy-start.32 = (f32[8,2]{0,1:T(2,128)S(1)}, f32[8,2]{0,1:T(2,128)}, u32[]{:S(2)}) copy-start(f32[8,2]{0,1:T(2,128)} %copy-done.31) | copy-start | bytes 196
  414.2 217.8 %copy-start.36 = (f32[8,2]{0,1:T(2,128)S(1)}, f32[8,2]{0,1:T(2,128)}, u32[]{:S(2)}) copy-start(f32[8,2]{0,1:T(2,128)} %get-tuple-element.261) | copy-start | bytes 196
  414.2 217.8 %copy-start.38 = (f32[8,2]{0,1:T(2,128)S(1)}, f32[8,2]{0,1:T(2,128)}, u32[]{:S(2)}) copy-start(f32[8,2]{0,1:T(2,128)} %get-tuple-element.238) | copy-start | bytes 196
  414.2 218.1 %copy-start.34 = (bf16[8,2,4]{0,2,1:T(4,128)(2,1)S(1)}, bf16[8,2,4]{0,2,1:T(4,128)(2,1)}, u32[]{:S(2)}) copy-start(bf16[8,2,4]{0,2,1:T(4,128)(2,1)} %get-tuple-element.239) | copy-start | bytes 388
  415.6 260.5 %copy-start.5 = (bf16[8,512,2,64]{1,0,3,2:T(8,128)(2,1)S(1)}, bf16[8,512,2,64]{1,0,3,2:T(8,128)(2,1)}, u32[]{:S(2)}) copy-start(bf16[8,512,2,64]{1,0,3,2:T(8,128)(2,1)} %get-tuple-element.250) | copy-start | bytes 3145732
  415.6 260.5 %copy-start.24 = (bf16[8,2,512,1]{2,0,1,3:T(8,128)(2,1)S(1)}, bf16[8,2,512,1]{2,0,1,3:T(8,128)(2,1)}, u32[]{:S(2)}) copy-start(bf16[8,2,512,1]{2,0,1,3:T(8,128)(2,1)} %get-tuple-element.262) | copy-start | bytes 49156
  545.2 131.5 %copy-start.27 = (bf16[8,4,2,64]{3,2,0,1:T(2,128)(2,1)S(1)}, bf16[8,4,2,64]{3,2,0,1:T(2,128)(2,1)}, u32[]{:S(2)}) copy-start(bf16[8,4,2,64]{3,2,0,1:T(2,128)(2,1)} %get-tuple-element.269) | copy-start | bytes 24580
  545.2 131.7 %copy-start.17 = (bf16[8,2,2,64]{3,2,1,0:T(2,128)(2,1)S(1)}, bf16[8,2,2,64]{3,2,1,0:T(2,128)(2,1)}, u32[]{:S(2)}) copy-start(bf16[8,2,2,64]{3,2,1,0:T(2,128)(2,1)} %copy-done.16) | copy-start | bytes 12292
  545.9 132.0 %copy-start.35 = (s32[8,4,1]{0,1,2:T(4,128)S(1)}, s32[8,4,1]{0,1,2:T(4,128)}, u32[]{:S(2)}) copy-start(s32[8,4,1]{0,1,2:T(4,128)} %get-tuple-element.299) | copy-start | bytes 388
  689.4 1.5 copy-start.25
  690.9 129.2 %copy-start.6 = (bf16[8,512,2,64]{1,0,3,2:T(8,128)(2,1)S(1)}, bf16[8,512,2,64]{1,0,3,2:T(8,128)(2,1)}, u32[]{:S(2)}) copy-start(bf16[8,512,2,64]{1,0,3,2:T(8,128)(2,1)} %get-tuple-element.252) | copy-start | bytes 3145732
  820.7 2.8 copy-start.37
  820.7 76.7 %copy-start.7 = (bf16[4,8,2048]{2,1,0:T(8,128)(2,1)S(1)}, bf16[4,8,2048]{2,1,0:T(8,128)(2,1)}, u32[]{:S(2)}) copy-start(bf16[4,8,2048]{2,1,0:T(8,128)(2,1)} %param.22) | copy-start | bytes 393220
  897.5 2.5 copy-start.11
  897.5 3.1 copy-start.10
  900.0 1.1 copy-start.9
Sparse Core Ops, SparseCore 0:
  821.9 75.5 all-reduce.3
where the time goes:
time: 916 us; the launch traced here: 910 us
  blocking collectives  706 us (77%)
  local copies, waits for them, and re-layouts  74.7 us (8%)
  waiting for transfers between devices  73.9 us (8%)
  matrix products  21.2 us (2%)
  other arithmetic  17.5 us (2%)
  between operations  16.8 us (2%)
    all_gather x4, blocking collectives, shards(): all_queries = lax.all_gather(query_block, 'req', axis=1, tiled=True)  200 us
    all_gather x4, blocking collectives, shards(): all_numer = lax.all_gather(held_numer, 'req', axis=1, tiled=True)  170 us
    all_gather x4, blocking collectives, shards(): all_top = lax.all_gather(held_top, 'req', axis=1, tiled=True)  168 us
    all_gather x4, blocking collectives, shards(): all_sum_rows = lax.all_gather(held_sum, 'req', axis=1, tiled=True)  168 us
    psum x1, waiting for transfers between devices, shards(): head_total = lax.psum(projected, 'tp')  73.9 us
    gather x8, local copies, waits for them, and re-layouts, shards(): home_cache[tables].reshape(row_count, home_tokens, 2, head_count, HEAD_DIM)  33.7 us
  transfers between devices with their start and end apart: 1, of which 1 were waited for; matrix products, arithmetic and copies ran while one was open for 0% of the time, Pallas kernels for 0%

commit v1 on v0

--- a/solution.py
+++ b/solution.py
@@ -3,6 +3,7 @@
 import jax.numpy as jnp
 from jax import lax
 from jax.sharding import PartitionSpec as P
+from jax.lax import all_gather
 
 HEAD_DIM = 64
 BEAMS = 8
@@ -86,8 +87,14 @@
         held_top = row_top.reshape(prompt_block_steps, row_count, head_count)
         held_sum = weight_sum.reshape(prompt_block_steps, row_count, head_count)
         all_numer = lax.all_gather(held_numer, "req", axis=1, tiled=True)
-        all_top = lax.all_gather(held_top, "req", axis=1, tiled=True)
-        all_sum_rows = lax.all_gather(held_sum, "req", axis=1, tiled=True)
+        convert_series_all_by_axis = lambda t0, along_axis, content: jnp.split(
+            all_gather(
+                jnp.concatenate([t0, content], axis=0), axis_name=along_axis, axis=1, tiled=True
+            ),
+            [t0.shape[0]],
+            axis=0,
+        )
+        all_top, all_sum_rows = convert_series_all_by_axis(held_top, "req", held_sum)
         route_prompt_numer = all_numer.reshape(
             route_block_steps, req_size * request_count, BEAMS, lane_count
         )[:, prompt_place].reshape(route_block_steps, row_count, lane_count)

time: 916 us -> 760 us (0.83)
  blocking collectives: 706 us -> 564 us
  other arithmetic: 17.5 us -> 6.92 us
    all_gather x8 -> x4, blocking collectives: 336 us -> 197 us  [shards(): all_gather(jnp.concatenate([t0, content], axis=0), axis_name=along_axis,...]
where the time goes in v1:
time: 760 us; the launch traced here: 751 us
  blocking collectives  564 us (74%)
  waiting for transfers between devices  73.9 us (10%)
  local copies, waits for them, and re-layouts  70.7 us (9%)
  matrix products  19.1 us (3%)
  between operations  16.7 us (2%)
    all_gather x4, blocking collectives, shards(): all_queries = lax.all_gather(query_block, 'req', axis=1, tiled=True)  200 us
    all_gather x4, blocking collectives, shards(): all_gather(jnp.concatenate([t0, content], axis=0), axis_name=along_axis,...  197 us
    all_gather x4, blocking collectives, shards(): all_numer = lax.all_gather(held_numer, 'req', axis=1, tiled=True)  167 us
    psum x1, waiting for transfers between devices, shards(): head_total = lax.psum(projected, 'tp')  73.9 us
    gather x8, local copies, waits for them, and re-layouts, shards(): home_cache[tables].reshape(row_count, home_tokens, 2, head_count, HEAD_DIM)  33.7 us
  transfers between devices with their start and end apart: 1, of which 1 were waited for; matrix products, arithmetic and copies ran while one was open for 0% of the time, Pallas kernels for 0%

profile of v1, /device:TPU:2, one launch (start us, length us, event | category | flops | bytes accessed | tf_op | source)
XLA Modules:
  0.0 751.0 jit_solution(12247263491195375339)
XLA Ops:
  7.2 0.8 fusion.140
  8.2 0.8 fusion.117
  9.0 0.8 copy.168
  12.4 6.4 gather_fusion.9
  18.8 2.8 copy.198
  21.6 3.1 reshape.675
  24.7 1.4 slice_bitcast_fusion.3
  29.6 1.9 fusion.22
  32.5 55.4 %all_gather.42 = bf16[1,512,128]{2,1,0:T(8,128)(2,1)S(1)} all-gather(bf16[1,8,128]{2,1,0:T(8,128)(2,1)S(1)} %get-tuple-element.284), channel_id=1, replica_groups=mesh['req'=64,'tp'=8] {'req'}, dimensions={1}, use_global_device_ids=true | all-gather | bytes 133120 | tf_op jit(solution)/shard_map/all_gather | solution.py:61
  89.4 47.8 %all_gather.45 = bf16[1,512,128]{2,1,0:T(8,128)(2,1)S(1)} all-gather(bf16[1,8,128]{2,1,0:T(8,128)(2,1)S(1)} %get-tuple-element.287), channel_id=1, replica_groups=mesh['req'=64,'tp'=8] {'req'}, dimensions={1}, use_global_device_ids=true | all-gather | bytes 133120 | tf_op jit(solution)/shard_map/all_gather | solution.py:61
  139.9 5.4 gather_fusion.13
  145.3 2.8 copy.210
  148.1 3.1 reshape.687
  151.2 1.4 slice_bitcast_fusion.1
  153.4 1.9 fusion.18
  157.0 48.6 %all_gather.39 = bf16[1,512,128]{2,1,0:T(8,128)(2,1)S(1)} all-gather(bf16[1,8,128]{2,1,0:T(8,128)(2,1)S(1)} %get-tuple-element.285), channel_id=1, replica_groups=mesh['req'=64,'tp'=8] {'req'}, dimensions={1}, use_global_device_ids=true | all-gather | bytes 133120 | tf_op jit(solution)/shard_map/all_gather | solution.py:61
  206.1 5.4 gather_fusion.5
  211.5 2.8 copy.186
  214.3 3.1 reshape.663
  217.4 1.1 slice_bitcast_fusion.5
  218.5 0.7 fusion.26
  220.1 47.8 %all_gather.36 = bf16[1,512,128]{2,1,0:T(8,128)(2,1)S(1)} all-gather(bf16[1,8,128]{2,1,0:T(8,128)(2,1)S(1)} %get-tuple-element.286), channel_id=1, replica_groups=mesh['req'=64,'tp'=8] {'req'}, dimensions={1}, use_global_device_ids=true | all-gather | bytes 133120 | tf_op jit(solution)/shard_map/all_gather | solution.py:61
  269.8 48.7 %all_gather.43 = f32[2,512,2]{2,0,1:T(2,128)S(1)} all-gather(f32[2,8,2]{2,0,1:T(2,128)S(1)} %copy.201), channel_id=1, replica_groups=mesh['req'=64,'tp'=8] {'req'}, dimensions={1}, use_global_device_ids=true | all-gather | bytes 8320 | tf_op jit(solution)/shard_map/all_gather | solution.py:91
  319.6 41.7 %all_gather.44 = f32[1,512,128]{2,1,0:T(8,128)S(1)} all-gather(f32[1,8,128]{2,1,0:T(8,128)S(1)} %reshape.684), channel_id=1, replica_groups=mesh['req'=64,'tp'=8] {'req'}, dimensions={1}, use_global_device_ids=true | all-gather | bytes 266240 | tf_op jit(solution)/shard_map/all_gather | solution.py:89
  361.4 0.7 fusion.20
  362.5 49.5 %all_gather.46 = f32[2,512,2]{2,0,1:T(2,128)S(1)} all-gather(f32[2,8,2]{2,0,1:T(2,128)S(1)} %copy.213), channel_id=1, replica_groups=mesh['req'=64,'tp'=8] {'req'}, dimensions={1}, use_global_device_ids=true | all-gather | bytes 8320 | tf_op jit(solution)/shard_map/all_gather | solution.py:91
  413.1 41.7 %all_gather.47 = f32[1,512,128]{2,1,0:T(8,128)S(1)} all-gather(f32[1,8,128]{2,1,0:T(8,128)S(1)} %reshape.696), channel_id=1, replica_groups=mesh['req'=64,'tp'=8] {'req'}, dimensions={1}, use_global_device_ids=true | all-gather | bytes 266240 | tf_op jit(solution)/shard_map/all_gather | solution.py:89
  454.9 0.7 fusion.16
  455.9 0.8 fusion.147
  456.7 0.8 fusion.148
  457.6 49.3 %all_gather.40 = f32[2,512,2]{2,0,1:T(2,128)S(1)} all-gather(f32[2,8,2]{2,0,1:T(2,128)S(1)} %copy.189), channel_id=1, replica_groups=mesh['req'=64,'tp'=8] {'req'}, dimensions={1}, use_global_device_ids=true | all-gather | bytes 8320 | tf_op jit(solution)/shard_map/all_gather | solution.py:91
  508.1 41.7 %all_gather.41 = f32[1,512,128]{2,1,0:T(8,128)S(1)} all-gather(f32[1,8,128]{2,1,0:T(8,128)S(1)} %reshape.672), channel_id=1, replica_groups=mesh['req'=64,'tp'=8] {'req'}, dimensions={1}, use_global_device_ids=true | all-gather | bytes 266240 | tf_op jit(solution)/shard_map/all_gather | solution.py:89
  549.9 0.7 fusion.24
  550.9 0.8 fusion.146
  551.8 49.5 %all_gather.37 = f32[2,512,2]{2,0,1:T(2,128)S(1)} all-gather(f32[2,8,2]{2,0,1:T(2,128)S(1)} %copy.176), channel_id=1, replica_groups=mesh['req'=64,'tp'=8] {'req'}, dimensions={1}, use_global_device_ids=true | all-gather | bytes 8320 | tf_op jit(solution)/shard_map/all_gather | solution.py:91
  602.1 5.4 gather_fusion.2
  607.5 2.8 copy.171
  610.3 3.1 reshape.649
  613.4 1.5 slice_bitcast_fusion.7
  615.1 1.9 fusion.30
  618.0 41.7 %all_gather.38 = f32[1,512,128]{2,1,0:T(8,128)S(1)} all-gather(f32[1,8,128]{2,1,0:T(8,128)S(1)} %reshape.659), channel_id=1, replica_groups=mesh['req'=64,'tp'=8] {'req'}, dimensions={1}, use_global_device_ids=true | all-gather | bytes 266240 | tf_op jit(solution)/shard_map/all_gather | solution.py:89
  659.8 1.9 fusion.28
  661.9 0.8 fusion.145
  662.8 1.7 copy.183
  664.5 73.9 %all-reduce.4.cloned.1.call-done = (f32[8,2048]{1,0:T(8,128)}, f32[8,2048]{1,0:T(8,128)}, f32[8,2048]{1,0:T(8,128)}, f32[8,2048]{1,0:T(8,128)}) async-done(((f32[8,2048]{1,0:T(8,128)}, f32[8,2048]{1,0:T(8,128)}, f32[8,2048]{1,0:T(8,128)}, f32[8,2048]{1,0:T(8,128)}), (f32[8,2048]{1,0:T(8,128)}, f32[8,2048]{1,0:T(8,128)}, f32[8,2048]{1,0:T(8,128)}, f32[8,2048]{1,0:T(8,128)})) %all-reduce.4.cloned.1.call-update) | async-done | bytes 262160 | tf_op jit(solution)/shard_map/psum | solution.py:180
  738.5 1.1 multiply_reduce_fusion.3
  739.6 1.3 fusion.12
  742.6 0.7 pad_maximum_fusion
  (232 shorter events, 24.4 us)
Async XLA Ops:
  7.2 448.8 %copy-start = (bf16[128,2048]{1,0:T(8,128)(2,1)S(1)}, bf16[128,2048]{1,0:T(8,128)(2,1)}, u32[]{:S(2)}) copy-start(bf16[128,2048]{1,0:T(8,128)(2,1)} %param.31) | copy-start | bytes 1572868
  7.2 731.3 %all-reduce.4.cloned.1.call-start = ((), (), s32[]{:S(2)}) async-start(), calls=%async_computation | async-start | bytes 524288 | tf_op jit(solution)/shard_map/psum | solution.py:180
  24.7 1.5 copy-start.1
  24.7 3.5 copy-start.11
  26.8 110.5 %copy-start.7 = (bf16[4,128,2,128]{3,2,1,0:T(2,128)(2,1)S(1)}, bf16[4,128,2,128]{3,2,1,0:T(2,128)(2,1)}, u32[]{:S(2)}) copy-start(bf16[4,128,2,128]{3,2,1,0:T(2,128)(2,1)} %param.24) | copy-start | bytes 786436
  29.6 110.3 %copy-start.2 = (bf16[4,128,2,128]{3,2,1,0:T(2,128)(2,1)S(1)}, bf16[4,128,2,128]{3,2,1,0:T(2,128)(2,1)}, u32[]{:S(2)}) copy-start(bf16[4,128,2,128]{3,2,1,0:T(2,128)(2,1)} %param.23) | copy-start | bytes 786436
  219.2 142.2 %copy-start.3 = (bf16[8,512,2,64]{1,0,3,2:T(8,128)(2,1)S(1)}, bf16[8,512,2,64]{1,0,3,2:T(8,128)(2,1)}, u32[]{:S(2)}) copy-start(bf16[8,512,2,64]{1,0,3,2:T(8,128)(2,1)} %get-tuple-element.246) | copy-start | bytes 3145732
  318.9 136.0 %copy-start.4 = (bf16[8,512,2,64]{1,0,3,2:T(8,128)(2,1)S(1)}, bf16[8,512,2,64]{1,0,3,2:T(8,128)(2,1)}, u32[]{:S(2)}) copy-start(bf16[8,512,2,64]{1,0,3,2:T(8,128)(2,1)} %get-tuple-element.248) | copy-start | bytes 3145732
  454.9 95.0 %copy-start.5 = (bf16[8,512,2,64]{1,0,3,2:T(8,128)(2,1)S(1)}, bf16[8,512,2,64]{1,0,3,2:T(8,128)(2,1)}, u32[]{:S(2)}) copy-start(bf16[8,512,2,64]{1,0,3,2:T(8,128)(2,1)} %get-tuple-element.250) | copy-start | bytes 3145732
  661.7 2.8 copy-start.12
  661.7 76.7 %copy-start.6 = (bf16[4,8,2048]{2,1,0:T(8,128)(2,1)S(1)}, bf16[4,8,2048]{2,1,0:T(8,128)(2,1)}, u32[]{:S(2)}) copy-start(bf16[4,8,2048]{2,1,0:T(8,128)(2,1)} %param.22) | copy-start | bytes 393220
  738.4 2.5 copy-start.10
  738.4 3.1 copy-start.9
  741.0 1.1 copy-start.8
Sparse Core Ops, SparseCore 0:
  662.9 75.5 all-reduce.3
